TPU v7x, 32 devices: a whole 2x2x4 slice. The times are simulated.
32 devices in a mesh: freq: 4 (over y, core), tcol: 8 (over z, x).
Axes of the slice: x: 2, y: 2, z: 4, core: 2. Of those that a mesh axis runs over, the one named last changes fastest.
Arguments:
- data: bfloat16 [4, 2, 4096, 128], P('freq', None, 'tcol'), may hold values from -6 to 6
- left_factor: bfloat16 [4, 2, 4096, 256], P('freq', None, 'tcol'), may hold values from -0.25 to 0.25
- right_factor: bfloat16 [4, 2, 4096, 256], P('freq', None, 'tcol'), may hold values from -0.1875 to 0.1875
- ranks: int32 [4, 8, 8], P('freq'), may hold values from 1 to 32
- freq_index: int32 [4], P('freq'), may hold values from 0 to 229
Outputs:
- wavefield: float32 [4, 2, 4096, 128], P('freq', None, 'tcol')
- residual: float32 [4, 2, 4096, 128], P('freq', None, 'tcol')
Inputs may be any that keep to these rules, and one draw needn't show every extreme that they name: `ranks`: the rank of each tile; factor columns at or beyond it are not part of the kernel.
All inputs are finite; a program needn't handle non-finite values.
Results may differ from a plain program's by a relative error of at most 0.006.
Values may be sent and summed in bfloat16 or wider, within the bound.
No kernel may reach another device: no remote copies, remote signals or barrier semaphores. Data moves between devices by JAX's collectives and lax.ppermute only.
A program may use at most 64 MiB of HBM per device.

v0:
```python
import jax
import jax.numpy as jnp
from jax import lax
from jax.sharding import PartitionSpec as P

ITERS = 3


def conj_left(factor, field):
    first = jnp.einsum(
        "ftq,fts->fqs", factor[:, 0], field[:, 0], preferred_element_type=jnp.float32
    )
    second = jnp.einsum(
        "ftq,fts->fqs", factor[:, 1], field[:, 1], preferred_element_type=jnp.float32
    )
    third = jnp.einsum(
        "ftq,fts->fqs", factor[:, 0], field[:, 1], preferred_element_type=jnp.float32
    )
    fourth = jnp.einsum(
        "ftq,fts->fqs", factor[:, 1], field[:, 0], preferred_element_type=jnp.float32
    )
    return jnp.stack([first + second, third - fourth], 1)


def plain_right(factor, coeffs):
    first = jnp.einsum(
        "ftq,fqs->fts", factor[:, 0], coeffs[:, 0], preferred_element_type=jnp.float32
    )
    second = jnp.einsum(
        "ftq,fqs->fts", factor[:, 1], coeffs[:, 1], preferred_element_type=jnp.float32
    )
    third = jnp.einsum(
        "ftq,fqs->fts", factor[:, 0], coeffs[:, 1], preferred_element_type=jnp.float32
    )
    fourth = jnp.einsum(
        "ftq,fqs->fts", factor[:, 1], coeffs[:, 0], preferred_element_type=jnp.float32
    )
    return jnp.stack([first - second, third + fourth], 1)


def body(data, left_factor, right_factor, ranks, freq_index):
    ntile = lax.axis_size("tcol")
    here = lax.axis_index("tcol")
    rank_width = left_factor.shape[3] // ntile
    levels = jnp.arange(rank_width)[None, None, :]
    column_ranks = lax.dynamic_slice_in_dim(ranks, here, 1, 2)[:, :, 0]
    row_ranks = lax.dynamic_slice_in_dim(ranks, here, 1, 1)[:, 0, :]
    colmask = (levels < column_ranks[:, :, None]).astype(jnp.float32).reshape(ranks.shape[0], -1)
    rowmask = (levels < row_ranks[:, :, None]).astype(jnp.float32).reshape(ranks.shape[0], -1)
    damping = (0.1 + 0.9 * freq_index.astype(jnp.float32) / 229.0)[:, None, None, None]
    residual = data.astype(jnp.float32)
    wavefield = jnp.zeros_like(residual)
    direction = jnp.zeros_like(residual)
    image = jnp.zeros_like(residual)
    for step in range(ITERS):
        coeffs = conj_left(left_factor, residual.astype(jnp.bfloat16))
        coeffs = (coeffs * rowmask[:, None, :, None]).astype(jnp.bfloat16)
        arrived = lax.all_to_all(coeffs, "tcol", split_axis=2, concat_axis=2, tiled=True)
        gradient = plain_right(right_factor, arrived) - damping * wavefield
        forward_coeffs = conj_left(right_factor, gradient.astype(jnp.bfloat16))
        forward_coeffs = (forward_coeffs * colmask[:, None, :, None]).astype(jnp.bfloat16)
        forward_arrived = lax.all_to_all(
            forward_coeffs, "tcol", split_axis=2, concat_axis=2, tiled=True
        )
        moved = plain_right(left_factor, forward_arrived)
        partial_sums = jnp.stack(
            [
                jnp.sum(moved * moved + damping * gradient * gradient, axis=(0, 1, 2)),
                jnp.sum(moved * image + damping * gradient * direction, axis=(0, 1, 2)),
                jnp.sum(image * image + damping * direction * direction, axis=(0, 1, 2)),
                jnp.sum(moved * residual - damping * gradient * wavefield, axis=(0, 1, 2)),
                jnp.sum(image * residual - damping * direction * wavefield, axis=(0, 1, 2)),
            ]
        )
        totals = lax.psum(partial_sums, ("freq", "tcol"))
        a11, a12, a22, b1, b2 = (totals[0], totals[1], totals[2], totals[3], totals[4])
        if step == 0:
            alpha = b1 / (1.1 * a11)
            beta = jnp.zeros_like(alpha)
        else:
            first = 1.1 * a11
            second = 1.1 * a22
            determinant = first * second - a12 * a12
            alpha = (b1 * second - a12 * b2) / determinant
            beta = (first * b2 - a12 * b1) / determinant
        direction = alpha * gradient + beta * direction
        image = alpha * moved + beta * image
        wavefield = wavefield + direction
        residual = residual - image
    return (wavefield, residual)


def solution(mesh):
    in_specs = (
        P("freq", None, "tcol", None),
        P("freq", None, "tcol", None),
        P("freq", None, "tcol", None),
        P("freq", None, None),
        P("freq"),
    )
    out_specs = (P("freq", None, "tcol", None), P("freq", None, "tcol", None))
    return jax.shard_map(body, mesh=mesh, in_specs=in_specs, out_specs=out_specs, check_vma=False)
```

profile of v0, /device:TPU:0, one launch (start us, length us, event | category | flops | bytes accessed | tf_op | source)
XLA Modules:
  0.0 213.9 jit_solution(10456277240478988102)
XLA Ops:
  0.7 0.7 copy-done
  1.5 1.2 fusion.116
  2.8 1.2 fusion.118
  4.4 0.3 fusion.22
  4.7 0.3 fusion.23
  5.1 0.8 copy.35
  5.9 7.3 %all-to-all-start = ((bf16[1,2,256,128]{3,1,0,2:T(2,128)(2,1)}), bf16[1,2,256,128]{3,1,0,2:T(2,128)(2,1)S(1)}, u32[]{:S(2)}, u32[]{:S(2)}) async-start(bf16[1,2,256,128]{3,1,0,2:T(2,128)(2,1)} %copy.35), calls=%async_computation | async-start | bytes 262144 | tf_op jit(solution)/shard_map/all_to_all | solution.py:58
  13.8 6.7 %all-to-all-done = bf16[1,2,256,128]{3,1,0,2:T(2,128)(2,1)S(1)} async-done(((bf16[1,2,256,128]{3,1,0,2:T(2,128)(2,1)}), bf16[1,2,256,128]{3,1,0,2:T(2,128)(2,1)S(1)}, u32[]{:S(2)}, u32[]{:S(2)}) %all-to-all-start) | async-done | bytes 131104 | tf_op jit(solution)/shard_map/all_to_all | solution.py:58
  21.1 0.2 fusion.11
  21.4 0.2 fusion.10
  22.5 0.8 copy.38
  23.3 3.4 %all-to-all-start.1 = ((bf16[1,2,256,128]{3,1,0,2:T(2,128)(2,1)}), bf16[1,2,256,128]{3,1,0,2:T(2,128)(2,1)S(1)}, u32[]{:S(2)}, u32[]{:S(2)}) async-start(bf16[1,2,256,128]{3,1,0,2:T(2,128)(2,1)} %copy.38), calls=%async_computation.1 | async-start | bytes 262144 | tf_op jit(solution)/shard_map/all_to_all | solution.py:62
  26.8 7.1 %all-to-all-done.1 = bf16[1,2,256,128]{3,1,0,2:T(2,128)(2,1)S(1)} async-done(((bf16[1,2,256,128]{3,1,0,2:T(2,128)(2,1)}), bf16[1,2,256,128]{3,1,0,2:T(2,128)(2,1)S(1)}, u32[]{:S(2)}, u32[]{:S(2)}) %all-to-all-start.1) | async-done | bytes 131104 | tf_op jit(solution)/shard_map/all_to_all | solution.py:62
  34.6 0.2 fusion.9
  34.8 0.2 fusion.8
  35.1 0.4 fusion.39
  35.5 38.5 %psum.21 = f32[5,128]{1,0:T(8,128)S(1)} all-reduce(f32[5,128]{1,0:T(8,128)S(1)} %stack.179), channel_id=1, replica_groups=mesh['freq'=4,'tcol'=8] {'freq','tcol'}, use_global_device_ids=true, to_apply=%region_4.0 | all-reduce | flops 640 | bytes 5120 | tf_op jit(solution)/shard_map/psum | solution.py:75
  74.2 0.3 fusion.108
  74.5 0.3 fusion.110
  74.7 0.3 fusion.18
  75.0 0.3 fusion.19
  75.5 11.7 %all_to_all.30 = bf16[1,2,256,128]{3,1,0,2:T(2,128)(2,1)S(1)} all-to-all(bf16[1,2,256,128]{3,1,0,2:T(2,128)(2,1)S(1)} %copy.46), channel_id=1, replica_groups=mesh['freq'=4,'tcol'=8] {'tcol'}, dimensions={2} | all-to-all | bytes 262144 | tf_op jit(solution)/shard_map/all_to_all | solution.py:58
  87.9 0.2 fusion.7
  88.1 0.2 fusion.6
  89.5 9.7 %all_to_all.31 = bf16[1,2,256,128]{3,1,0,2:T(2,128)(2,1)S(1)} all-to-all(bf16[1,2,256,128]{3,1,0,2:T(2,128)(2,1)S(1)} %copy.49), channel_id=1, replica_groups=mesh['freq'=4,'tcol'=8] {'tcol'}, dimensions={2} | all-to-all | bytes 262144 | tf_op jit(solution)/shard_map/all_to_all | solution.py:62
  99.9 0.2 fusion.5
  100.1 0.2 fusion.4
  100.4 0.3 add_reduce_fusion.1
  100.8 0.3 copy-done.6
  101.0 0.6 subtract_reduce_fusion
  101.7 38.3 %psum.22 = f32[5,128]{1,0:T(8,128)S(1)} all-reduce(f32[5,128]{1,0:T(8,128)S(1)} %stack.197), channel_id=1, replica_groups=mesh['freq'=4,'tcol'=8] {'freq','tcol'}, use_global_device_ids=true, to_apply=%region_10.0 | all-reduce | flops 640 | bytes 5120 | tf_op jit(solution)/shard_map/psum | solution.py:75
  139.9 2.1 fusion.186
  142.0 0.3 fusion.100
  142.3 0.3 fusion.102
  142.5 0.3 fusion.14
  142.8 0.3 fusion.15
  143.3 11.7 %all_to_all.32 = bf16[1,2,256,128]{3,1,0,2:T(2,128)(2,1)S(1)} all-to-all(bf16[1,2,256,128]{3,1,0,2:T(2,128)(2,1)S(1)} %copy.56), channel_id=1, replica_groups=mesh['freq'=4,'tcol'=8] {'tcol'}, dimensions={2} | all-to-all | bytes 262144 | tf_op jit(solution)/shard_map/all_to_all | solution.py:58
  156.2 1.1 fusion.185
  158.2 9.7 %all_to_all.33 = bf16[1,2,256,128]{3,1,0,2:T(2,128)(2,1)S(1)} all-to-all(bf16[1,2,256,128]{3,1,0,2:T(2,128)(2,1)S(1)} %copy.59), channel_id=1, replica_groups=mesh['freq'=4,'tcol'=8] {'tcol'}, dimensions={2} | all-to-all | bytes 262144 | tf_op jit(solution)/shard_map/all_to_all | solution.py:62
  168.6 0.2 fusion.1
  168.9 0.2 fusion
  169.1 0.5 copy-done.4
  169.7 0.3 copy-done.3
  169.9 0.7 fusion.37
  170.7 38.3 %psum.23 = f32[5,128]{1,0:T(8,128)S(1)} all-reduce(f32[5,128]{1,0:T(8,128)S(1)} %stack.215), channel_id=1, replica_groups=mesh['freq'=4,'tcol'=8] {'freq','tcol'}, use_global_device_ids=true, to_apply=%region_16.0 | all-reduce | flops 640 | bytes 5120 | tf_op jit(solution)/shard_map/psum | solution.py:75
  209.0 2.0 add_subtract_fusion
  210.9 2.0 copy.63
  213.0 1.0 copy.62
  (75 shorter events, 8.7 us)
Async XLA Ops:
  0.6 0.7 copy-start
  0.6 2.1 copy-start.2
  2.8 1.6 copy-start.8
  5.1 15.6 %copy-start.1 = (bf16[1,2,512,256]{3,2,1,0:T(8,128)(2,1)S(1)}, bf16[1,2,512,256]{3,2,1,0:T(8,128)(2,1)}, u32[]{:S(2)}) copy-start(bf16[1,2,512,256]{3,2,1,0:T(8,128)(2,1)} %param.7) | copy-start | bytes 1572868
  5.9 14.6 %all-to-all-start = ((bf16[1,2,256,128]{3,1,0,2:T(2,128)(2,1)}), bf16[1,2,256,128]{3,1,0,2:T(2,128)(2,1)S(1)}, u32[]{:S(2)}, u32[]{:S(2)}) async-start(bf16[1,2,256,128]{3,1,0,2:T(2,128)(2,1)} %copy.35), calls=%async_computation | async-start | bytes 262144 | tf_op jit(solution)/shard_map/all_to_all | solution.py:58
  23.3 10.7 %all-to-all-start.1 = ((bf16[1,2,256,128]{3,1,0,2:T(2,128)(2,1)}), bf16[1,2,256,128]{3,1,0,2:T(2,128)(2,1)S(1)}, u32[]{:S(2)}, u32[]{:S(2)}) async-start(bf16[1,2,256,128]{3,1,0,2:T(2,128)(2,1)} %copy.38), calls=%async_computation.1 | async-start | bytes 262144 | tf_op jit(solution)/shard_map/all_to_all | solution.py:62
  100.1 0.7 copy-start.5
  100.3 0.7 copy-start.6
  168.6 1.0 copy-start.4
  168.9 1.1 copy-start.3
  169.1 1.5 copy-start.7
where the time goes:
time: 215 us; the launch traced here: 214 us
  blocking collectives  158 us (73%)
  waiting for transfers between devices  13.8 us (6%)
  matrix products  13 us (6%)
  starting transfers between devices  10.7 us (5%)
  local copies, waits for them, and re-layouts  8.86 us (4%)
  other arithmetic  7.88 us (4%)
    psum x3, blocking collectives, body(): totals = lax.psum(partial_sums, ('freq', 'tcol'))  115 us
    all_to_all x2, blocking collectives, body(): lax.all_to_all(coeffs, 'tcol', split_axis=2, concat_axis=2, tiled=True)  23.4 us
    all_to_all x2, blocking collectives, body(): lax.all_to_all(forward_coeffs, 'tcol', split_axis=2, concat_axis=2, tiled...  19.5 us
    all_to_all x1, starting transfers between devices, body(): lax.all_to_all(coeffs, 'tcol', split_axis=2, concat_axis=2, tiled=True)  7.28 us
    all_to_all x1, waiting for transfers between devices, body(): lax.all_to_all(forward_coeffs, 'tcol', split_axis=2, concat_axis=2, tiled...  7.12 us
    all_to_all x1, waiting for transfers between devices, body(): lax.all_to_all(coeffs, 'tcol', split_axis=2, concat_axis=2, tiled=True)  6.69 us
    unnamed x21, local copies, waits for them, and re-layouts  5.08 us
  transfers between devices with their start and end apart: 2, of which 2 were waited for; matrix products, arithmetic and copies ran while one was open for 0% of the time, Pallas kernels for 0%

commit v1 on v0

--- a/solution.py
+++ b/solution.py
@@ -72,7 +72,8 @@
                 jnp.sum(image * residual - damping * direction * wavefield, axis=(0, 1, 2)),
             ]
         )
-        totals = lax.psum(partial_sums, ("freq", "tcol"))
+        partial = lax.psum(partial_sums, "tcol")
+        totals = lax.psum(partial, "freq")
         a11, a12, a22, b1, b2 = (totals[0], totals[1], totals[2], totals[3], totals[4])
         if step == 0:
             alpha = b1 / (1.1 * a11)

time: 215 us -> 168 us (0.78)
  blocking collectives: 158 us -> 111 us
    psum x3 -> x6, blocking collectives: 115 us -> 71.6 us  [the longest x3 54.6 us: body(): partial = lax.psum(partial_sums, 'tcol')]
    all_to_all x2, blocking collectives: 23.4 us -> 19.5 us  [body(): lax.all_to_all(coeffs, 'tcol', split_axis=2, concat_axis=2, tiled=True)]
where the time goes in v1:
time: 168 us; the launch traced here: 167 us
  blocking collectives  111 us (66%)
  waiting for transfers between devices  13.8 us (8%)
  matrix products  12.9 us (8%)
  starting transfers between devices  10.7 us (6%)
  local copies, waits for them, and re-layouts  8.86 us (5%)
  other arithmetic  7.89 us (5%)
  between operations  1.9 us (1%)
    psum x3, blocking collectives, body(): partial = lax.psum(partial_sums, 'tcol')  54.6 us
    all_to_all x2, blocking collectives, body(): lax.all_to_all(forward_coeffs, 'tcol', split_axis=2, concat_axis=2, tiled...  19.6 us
    all_to_all x2, blocking collectives, body(): lax.all_to_all(coeffs, 'tcol', split_axis=2, concat_axis=2, tiled=True)  19.5 us
    psum x3, blocking collectives, body(): totals = lax.psum(partial, 'freq')  17 us
    all_to_all x1, starting transfers between devices, body(): lax.all_to_all(coeffs, 'tcol', split_axis=2, concat_axis=2, tiled=True)  7.28 us
    all_to_all x1, waiting for transfers between devices, body(): lax.all_to_all(forward_coeffs, 'tcol', split_axis=2, concat_axis=2, tiled...  7.12 us
    all_to_all x1, waiting for transfers between devices, body(): lax.all_to_all(coeffs, 'tcol', split_axis=2, concat_axis=2, tiled=True)  6.69 us
    unnamed x21, local copies, waits for them, and re-layouts  5.08 us
  transfers between devices with their start and end apart: 2, of which 2 were waited for; matrix products, arithmetic and copies ran while one was open for 0% of the time, Pallas kernels for 0%

profile of v1, /device:TPU:0, one launch (start us, length us, event | category | flops | bytes accessed | tf_op | source)
XLA Modules:
  0.0 166.8 jit_solution(4391480301424513265)
XLA Ops:
  0.7 0.7 copy-done
  1.5 1.2 fusion.116
  2.8 1.2 fusion.118
  4.4 0.3 fusion.22
  4.7 0.3 fusion.23
  5.1 0.8 copy.35
  5.9 7.3 %all-to-all-start = ((bf16[1,2,256,128]{3,1,0,2:T(2,128)(2,1)}), bf16[1,2,256,128]{3,1,0,2:T(2,128)(2,1)S(1)}, u32[]{:S(2)}, u32[]{:S(2)}) async-start(bf16[1,2,256,128]{3,1,0,2:T(2,128)(2,1)} %copy.35), calls=%async_computation | async-start | bytes 262144 | tf_op jit(solution)/shard_map/all_to_all | solution.py:58
  13.8 6.7 %all-to-all-done = bf16[1,2,256,128]{3,1,0,2:T(2,128)(2,1)S(1)} async-done(((bf16[1,2,256,128]{3,1,0,2:T(2,128)(2,1)}), bf16[1,2,256,128]{3,1,0,2:T(2,128)(2,1)S(1)}, u32[]{:S(2)}, u32[]{:S(2)}) %all-to-all-start) | async-done | bytes 131104 | tf_op jit(solution)/shard_map/all_to_all | solution.py:58
  21.1 0.2 fusion.11
  22.5 0.8 copy.38
  23.3 3.4 %all-to-all-start.1 = ((bf16[1,2,256,128]{3,1,0,2:T(2,128)(2,1)}), bf16[1,2,256,128]{3,1,0,2:T(2,128)(2,1)S(1)}, u32[]{:S(2)}, u32[]{:S(2)}) async-start(bf16[1,2,256,128]{3,1,0,2:T(2,128)(2,1)} %copy.38), calls=%async_computation.1 | async-start | bytes 262144 | tf_op jit(solution)/shard_map/all_to_all | solution.py:62
  26.8 7.1 %all-to-all-done.1 = bf16[1,2,256,128]{3,1,0,2:T(2,128)(2,1)S(1)} async-done(((bf16[1,2,256,128]{3,1,0,2:T(2,128)(2,1)}), bf16[1,2,256,128]{3,1,0,2:T(2,128)(2,1)S(1)}, u32[]{:S(2)}, u32[]{:S(2)}) %all-to-all-start.1) | async-done | bytes 131104 | tf_op jit(solution)/shard_map/all_to_all | solution.py:62
  34.6 0.2 fusion.9
  34.8 0.2 fusion.8
  35.1 0.4 fusion.39
  35.5 18.2 %psum.42 = f32[5,128]{1,0:T(8,128)S(1)} all-reduce(f32[5,128]{1,0:T(8,128)S(1)} %stack.179), channel_id=1, replica_groups=mesh['freq'=4,'tcol'=8] {'tcol'}, use_global_device_ids=true, to_apply=%region_4.0 | all-reduce | flops 640 | bytes 5120 | tf_op jit(solution)/shard_map/psum | solution.py:75
  53.7 5.7 %psum.43 = f32[5,128]{1,0:T(8,128)S(1)} all-reduce(f32[5,128]{1,0:T(8,128)S(1)} %psum.42), channel_id=1, replica_groups=mesh['freq'=4,'tcol'=8] {'freq'}, use_global_device_ids=true, to_apply=%region_5.0 | all-reduce | flops 640 | bytes 5120 | tf_op jit(solution)/shard_map/psum | solution.py:76
  59.5 0.3 fusion.108
  59.8 0.3 fusion.110
  60.1 0.3 fusion.18
  60.4 0.3 fusion.19
  60.9 9.7 %all_to_all.30 = bf16[1,2,256,128]{3,1,0,2:T(2,128)(2,1)S(1)} all-to-all(bf16[1,2,256,128]{3,1,0,2:T(2,128)(2,1)S(1)} %copy.46), channel_id=1, replica_groups=mesh['freq'=4,'tcol'=8] {'tcol'}, dimensions={2} | all-to-all | bytes 262144 | tf_op jit(solution)/shard_map/all_to_all | solution.py:58
  71.3 0.2 fusion.7
  72.9 9.8 %all_to_all.31 = bf16[1,2,256,128]{3,1,0,2:T(2,128)(2,1)S(1)} all-to-all(bf16[1,2,256,128]{3,1,0,2:T(2,128)(2,1)S(1)} %copy.49), channel_id=1, replica_groups=mesh['freq'=4,'tcol'=8] {'tcol'}, dimensions={2} | all-to-all | bytes 262144 | tf_op jit(solution)/shard_map/all_to_all | solution.py:62
  83.3 0.2 fusion.5
  83.8 0.3 add_reduce_fusion.1
  84.3 0.3 copy-done.6
  84.5 0.6 subtract_reduce_fusion
  85.1 18.2 %psum.44 = f32[5,128]{1,0:T(8,128)S(1)} all-reduce(f32[5,128]{1,0:T(8,128)S(1)} %stack.197), channel_id=1, replica_groups=mesh['freq'=4,'tcol'=8] {'tcol'}, use_global_device_ids=true, to_apply=%region_11.0 | all-reduce | flops 640 | bytes 5120 | tf_op jit(solution)/shard_map/psum | solution.py:75
  103.3 5.7 %psum.45 = f32[5,128]{1,0:T(8,128)S(1)} all-reduce(f32[5,128]{1,0:T(8,128)S(1)} %psum.44), channel_id=1, replica_groups=mesh['freq'=4,'tcol'=8] {'freq'}, use_global_device_ids=true, to_apply=%region_12.0 | all-reduce | flops 640 | bytes 5120 | tf_op jit(solution)/shard_map/psum | solution.py:76
  109.0 2.1 %fusion.186 = (bf16[1,2,512,128]{2,3,1,0:T(8,128)(2,1)S(1)}, f32[1,2,512,128]{2,3,1,0:T(8,128)S(1)}, f32[1,2,512,128]{2,3,1,0:T(8,128)}) fusion(f32[1,1,512,128]{2,3,1,0:T(8,128)S(1)} %fusion.8, f32[1,1,512,128]{2,3,1,0:T(8,128)S(1)} %fusion.9, f32[128]{0:T(128)S(1)} %fusion.128, bf16[1,2,512,128]{2,3,1,0:T(8,128)(2,1)S(1)} %copy.41, ...), kind=kLoop, calls=%fused_computation.284 | loop fusion | flops 1310720 | bytes 2622976 | tf_op jit(solution)/shard_map/convert_element_type | solution.py:56
  111.1 0.3 fusion.100
  111.3 0.3 fusion.102
  111.6 0.3 fusion.14
  111.9 0.3 fusion.15
  112.4 9.8 %all_to_all.32 = bf16[1,2,256,128]{3,1,0,2:T(2,128)(2,1)S(1)} all-to-all(bf16[1,2,256,128]{3,1,0,2:T(2,128)(2,1)S(1)} %copy.56), channel_id=1, replica_groups=mesh['freq'=4,'tcol'=8] {'tcol'}, dimensions={2} | all-to-all | bytes 262144 | tf_op jit(solution)/shard_map/all_to_all | solution.py:58
  123.3 1.1 fusion.185
  125.4 9.8 %all_to_all.33 = bf16[1,2,256,128]{3,1,0,2:T(2,128)(2,1)S(1)} all-to-all(bf16[1,2,256,128]{3,1,0,2:T(2,128)(2,1)S(1)} %copy.59), channel_id=1, replica_groups=mesh['freq'=4,'tcol'=8] {'tcol'}, dimensions={2} | all-to-all | bytes 262144 | tf_op jit(solution)/shard_map/all_to_all | solution.py:62
  135.9 0.2 fusion.1
  136.1 0.2 fusion
  136.4 0.5 copy-done.4
  136.9 0.3 copy-done.3
  137.2 0.7 fusion.37
  137.9 18.2 %psum.46 = f32[5,128]{1,0:T(8,128)S(1)} all-reduce(f32[5,128]{1,0:T(8,128)S(1)} %stack.215), channel_id=1, replica_groups=mesh['freq'=4,'tcol'=8] {'tcol'}, use_global_device_ids=true, to_apply=%region_18.0 | all-reduce | flops 640 | bytes 5120 | tf_op jit(solution)/shard_map/psum | solution.py:75
  156.1 5.7 %psum.47 = f32[5,128]{1,0:T(8,128)S(1)} all-reduce(f32[5,128]{1,0:T(8,128)S(1)} %psum.46), channel_id=1, replica_groups=mesh['freq'=4,'tcol'=8] {'freq'}, use_global_device_ids=true, to_apply=%region_19.0 | all-reduce | flops 640 | bytes 5120 | tf_op jit(solution)/shard_map/psum | solution.py:76
  161.8 2.0 %add_subtract_fusion = (f32[1,2,512,128]{2,3,1,0:T(8,128)}, f32[1,2,512,128]{2,3,1,0:T(8,128)S(1)}) fusion(f32[1,2,512,128]{2,3,1,0:T(8,128)S(1)} %get-tuple-element.25, f32[1,2,512,128]{2,3,1,0:T(8,128)S(1)} %copy-done.3, f32[128]{0:T(128)S(1)} %get-tuple-element.42, f32[128]{0:T(128)S(1)} %get-tuple-element.41, f32[1,1,512,128]{2,3,1,0:T(8,128)} %copy-done.7, ...), kind=kLoop, calls=%fused_computation.85 | loop fusion | flops 1703936 | bytes 4195844 | tf_op jit(solution)/shard_map/sub | solution.py:90
  163.8 2.0 %copy.63 = f32[1,2,512,128]{3,2,1,0:T(8,128)} copy(f32[1,2,512,128]{2,3,1,0:T(8,128)} %get-tuple-element.45) | data formatting | bytes 1048576
  165.8 1.0 copy.62
  (78 shorter events, 9.4 us)
Async XLA Ops:
  0.6 0.7 copy-start
  0.6 2.1 %copy-start.2 = (bf16[1,2,512,256]{3,2,1,0:T(8,128)(2,1)S(1)}, bf16[1,2,512,256]{3,2,1,0:T(8,128)(2,1)}, u32[]{:S(2)}) copy-start(bf16[1,2,512,256]{3,2,1,0:T(8,128)(2,1)} %param.6) | copy-start | bytes 1572868
  2.8 1.6 copy-start.8
  5.1 15.6 %copy-start.1 = (bf16[1,2,512,256]{3,2,1,0:T(8,128)(2,1)S(1)}, bf16[1,2,512,256]{3,2,1,0:T(8,128)(2,1)}, u32[]{:S(2)}) copy-start(bf16[1,2,512,256]{3,2,1,0:T(8,128)(2,1)} %param.7) | copy-start | bytes 1572868
  5.9 14.6 %all-to-all-start = ((bf16[1,2,256,128]{3,1,0,2:T(2,128)(2,1)}), bf16[1,2,256,128]{3,1,0,2:T(2,128)(2,1)S(1)}, u32[]{:S(2)}, u32[]{:S(2)}) async-start(bf16[1,2,256,128]{3,1,0,2:T(2,128)(2,1)} %copy.35), calls=%async_computation | async-start | bytes 262144 | tf_op jit(solution)/shard_map/all_to_all | solution.py:58
  23.3 10.7 %all-to-all-start.1 = ((bf16[1,2,256,128]{3,1,0,2:T(2,128)(2,1)}), bf16[1,2,256,128]{3,1,0,2:T(2,128)(2,1)S(1)}, u32[]{:S(2)}, u32[]{:S(2)}) async-start(bf16[1,2,256,128]{3,1,0,2:T(2,128)(2,1)} %copy.38), calls=%async_computation.1 | async-start | bytes 262144 | tf_op jit(solution)/shard_map/all_to_all | solution.py:62
  83.6 0.7 copy-start.5
  83.8 0.7 copy-start.6
  135.9 1.0 copy-start.4
  136.1 1.1 copy-start.3
  136.4 1.5 copy-start.7
